TPU v7x, 32 devices: a whole 2x2x4 slice. The times are simulated.
32 devices in a mesh: dp: 2 (over x), expert: 16 (over z, y, core).
Axes of the slice: x: 2, y: 2, z: 4, core: 2. Of those that a mesh axis runs over, the one named last changes fastest.
Arguments:
- q_latent: bfloat16 [128, 16, 576], P(('expert', 'dp')), may hold values from -48 to 48
- latent_cache: bfloat16 [128, 512, 576], P(('expert', 'dp')), may hold values from -10 to 10
- lengths: int32 [128], P(('expert', 'dp')), may hold values from 2 to 512
- residual: bfloat16 [128, 2048], P(('expert', 'dp')), may hold values from -6 to 6
- adapter_ids: int32 [128], P(('expert', 'dp')), may hold values from 0 to 31
- value_out: bfloat16 [8192, 2048], P('expert'), may hold values from -0.0625 to 0.0625
- adapter_down: bfloat16 [8192, 512], P('expert'), may hold values from -0.0625 to 0.0625
- adapter_up_factors: bfloat16 [512, 2048], P('expert'), may hold values from -1.5 to 1.5
- norm_gain: bfloat16 [2048], replicated, may hold values from 0.099609375 to 1.8984375
- expert_ids: int32 [128, 6], P('expert'), may hold values from 0 to 15, all different within a row; in each aligned block of 8 rows (0 to 7, 8 to 15, ...) at most 6 rows name the same one
- gate_weights: float32 [128, 6], P('expert'), may hold values from 0.05 to 0.5
- w_gate: bfloat16 [16, 2048, 1024], P('expert', None, 'dp'), may hold values from -0.125 to 0.125
- w_up: bfloat16 [16, 2048, 1024], P('expert', None, 'dp'), may hold values from -0.125 to 0.125
- w_down: bfloat16 [16, 2048, 1024], P('expert', None, 'dp'), may hold values from -0.1875 to 0.1875
Outputs:
- layer_out: bfloat16 [128, 2048], P(('expert', 'dp'))
Inputs may be any that keep to these rules, and one draw needn't show every extreme that they name: `expert_ids`: each row names 6 different experts. Requests e * 8 to e * 8 + 7 form aligned blocks; in each block no expert is named by more than 6 rows, and in some block an expert is named by exactly 6 rows.
All inputs are finite; a program needn't handle non-finite values.
Results may differ from a plain program's by a relative error of at most 0.008.
Values may be sent and summed in bfloat16 or wider, within the bound.
A program may use at most 64 MiB of HBM per device.

v0:
```python
import jax
import jax.numpy as jnp
from jax import lax
from jax.sharding import PartitionSpec as P

LAT = 512
ADAPTER_RANK = 16
SOFTMAX_SCALE = 192.0 ** (-0.5)
ADAPTER_SCALE = 2.0
EPSILON = 1e-06


def attend_one(query, latent_rows, length):
    scores = (
        lax.dot_general(
            query, latent_rows, (((1,), (1,)), ((), ())), preferred_element_type=jnp.float32
        )
        * SOFTMAX_SCALE
    )
    valid_mask = jnp.arange(latent_rows.shape[0], dtype=jnp.int32) < length
    scores = jnp.where(valid_mask[None, :], scores, -1e30)
    row_max = jnp.max(scores, axis=1, keepdims=True)
    raised = jnp.exp(scores - row_max)
    weights_bf = (raised / jnp.sum(raised, axis=1, keepdims=True)).astype(jnp.bfloat16)
    return jnp.dot(weights_bf, latent_rows[:, :LAT], preferred_element_type=jnp.float32).astype(
        jnp.bfloat16
    )


def expert_rows(tokens, gate_part, up_part, down_part):
    gate_act = jnp.dot(tokens, gate_part, preferred_element_type=jnp.float32)
    up_act = jnp.dot(tokens, up_part, preferred_element_type=jnp.float32)
    hidden_bf = (jax.nn.silu(gate_act) * up_act).astype(jnp.bfloat16)
    return lax.dot_general(
        hidden_bf, down_part, (((1,), (1,)), ((), ())), preferred_element_type=jnp.float32
    )


def local(
    q_latent,
    latent_cache,
    lengths,
    residual,
    adapter_ids,
    value_out,
    adapter_down,
    adapter_up_factors,
    norm_gain,
    expert_ids,
    gate_weights,
    w_gate,
    w_up,
    w_down,
):
    requests = residual.shape[0]
    model_width = residual.shape[1]
    head_count = q_latent.shape[1]
    latent_out = jax.vmap(attend_one)(q_latent, latent_cache, lengths).reshape(
        requests, head_count * LAT
    )
    pieces = lax.all_to_all(latent_out, "expert", split_axis=1, concat_axis=0, tiled=True)
    group_ids = lax.all_gather(adapter_ids, "expert", axis=0, tiled=True)
    group_rows = pieces.shape[0]
    adapters = adapter_down.shape[1] // ADAPTER_RANK
    owned_count = adapter_up_factors.shape[0] // ADAPTER_RANK
    down_projected_rows = jnp.dot(pieces, adapter_down, preferred_element_type=jnp.float32).reshape(
        group_rows, adapters, ADAPTER_RANK
    )
    chosen_adapters = group_ids[:, None] == jnp.arange(adapters, dtype=jnp.int32)[None, :]
    adapter_output = jnp.sum(
        jnp.where(chosen_adapters[:, :, None], down_projected_rows, 0.0), axis=1
    )
    adapter_down_rows = lax.psum(adapter_output, "expert")
    adapter_scaled_output = (ADAPTER_SCALE * adapter_down_rows).astype(jnp.bfloat16)
    first_owned = lax.axis_index("expert") * owned_count
    holder_mask = (
        group_ids[:, None] == first_owned + jnp.arange(owned_count, dtype=jnp.int32)[None, :]
    )
    spread_rows = jnp.where(
        holder_mask[:, :, None], adapter_scaled_output[:, None, :], jnp.zeros((), jnp.bfloat16)
    ).reshape(group_rows, owned_count * ADAPTER_RANK)
    attention = lax.psum_scatter(
        jnp.dot(pieces, value_out, preferred_element_type=jnp.float32)
        + jnp.dot(spread_rows, adapter_up_factors, preferred_element_type=jnp.float32),
        "expert",
        scatter_dimension=0,
        tiled=True,
    )
    residual_flow = residual.astype(jnp.float32) + attention
    inverse_rms = lax.rsqrt(
        jnp.mean(residual_flow * residual_flow, axis=1, keepdims=True) + EPSILON
    )
    normed = (residual_flow * inverse_rms * norm_gain.astype(jnp.float32)).astype(jnp.bfloat16)
    column = lax.all_gather(normed, "dp", axis=0, tiled=True)
    tokens = column.shape[0]
    top_count = expert_ids.shape[1]
    experts = lax.axis_size("expert") * w_gate.shape[0]
    share_size = max(1, 2 * requests * top_count // experts)
    dp_count = lax.axis_size("dp")
    slot_count = share_size * dp_count
    member = expert_ids[:, :, None] == jnp.arange(experts, dtype=jnp.int32)[None, None, :]
    flat_hits = member.reshape(tokens * top_count, experts).astype(jnp.int32)
    slot_rank = jnp.sum((jnp.cumsum(flat_hits, axis=0) - 1) * flat_hits, axis=1).reshape(
        tokens, top_count
    )
    placed = member[:, :, :, None] & (
        slot_rank[:, :, None, None] == jnp.arange(slot_count, dtype=jnp.int32)[None, None, None, :]
    )
    routing = jnp.any(placed, axis=1).reshape(tokens, experts * slot_count)
    combine = jnp.sum(jnp.where(placed, gate_weights[:, :, None, None], 0.0), axis=1).reshape(
        tokens, experts * slot_count
    )
    routing_rows = routing.T.astype(jnp.bfloat16)
    outgoing = (
        jnp.dot(routing_rows, column, preferred_element_type=jnp.float32)
        .astype(jnp.bfloat16)
        .reshape(experts, slot_count, model_width)
    )
    arrived = lax.all_to_all(outgoing, "expert", split_axis=0, concat_axis=0, tiled=True)
    produced = expert_rows(arrived.reshape(-1, model_width), w_gate[0], w_up[0], w_down[0])
    partial_value = produced.reshape(arrived.shape[0], arrived.shape[1], model_width)
    returned = lax.all_to_all(
        partial_value.astype(jnp.bfloat16), "expert", split_axis=0, concat_axis=0, tiled=True
    ).astype(partial_value.dtype)
    routed_column = jnp.dot(
        combine,
        returned.reshape(experts * slot_count, model_width),
        precision=lax.Precision.HIGHEST,
        preferred_element_type=jnp.float32,
    )
    routed_sum = lax.psum_scatter(
        routed_column.astype(jnp.bfloat16), "dp", scatter_dimension=0, tiled=True
    ).astype(jnp.float32)
    return (residual_flow + routed_sum).astype(jnp.bfloat16)


def solution(mesh):
    in_specs = (
        P(("expert", "dp"), None, None),
        P(("expert", "dp"), None, None),
        P(("expert", "dp")),
        P(("expert", "dp"), None),
        P(("expert", "dp")),
        P("expert", None),
        P("expert", None),
        P("expert", None),
        P(),
        P("expert", None),
        P("expert", None),
        P("expert", None, "dp"),
        P("expert", None, "dp"),
        P("expert", None, "dp"),
    )
    out_specs = P(("expert", "dp"), None)
    return jax.shard_map(local, mesh=mesh, in_specs=in_specs, out_specs=out_specs, check_vma=False)
```

profile of v0, /device:TPU:0, one launch (start us, length us, event | category | flops | bytes accessed | tf_op | source)
XLA Modules:
  0.0 223.4 jit_solution(10527450560244738211)
XLA Ops:
  6.5 0.0 copy-start
  6.5 0.9 iota_compare_fusion.4
  7.4 2.1 fusion.17
  9.6 0.0 copy-start.7
  9.6 0.0 copy-start.9
  9.6 0.0 copy-start.1
  9.6 0.0 copy-start.5
  9.6 0.2 fusion.31
  9.8 2.3 %fusion.19 = bf16[4,16,512]{2,1,0:T(8,128)(2,1)S(1)} fusion(bf16[4,512,576]{1,2,0:T(8,128)(2,1)} %param.15, f32[4,16]{1,0:T(4,128)S(1)} %fusion.31, f32[4,16,512]{2,1,0:T(8,128)S(1)} %fusion.17), kind=kOutput, calls=%fused_computation.21 | convolution fusion | flops 33686080 | bytes 2426880 | tf_op jit(solution)/shard_map/vmap()/dot_general | solution.py:25
  12.1 0.7 copy.29
  12.8 7.4 %all-to-all-start = ((bf16[4,16,512]{2,0,1:T(4,128)(2,1)}), bf16[4,16,512]{2,0,1:T(4,128)(2,1)S(1)}, u32[]{:S(2)}, u32[]{:S(2)}) async-start(bf16[4,16,512]{2,0,1:T(4,128)(2,1)} %copy.29), calls=%async_computation | async-start | bytes 131072 | tf_op jit(solution)/shard_map/all_to_all | solution.py:61
  20.2 0.0 all-reduce.5.cloned.1.call-start
  20.2 0.0 copy-done.4
  20.3 0.1 eq.89
  20.3 0.1 copy.32
  20.4 0.0 copy-done.7
  20.4 0.6 fusion.30
  21.7 0.2 dynamic-update-slice
  21.9 12.4 %all-reduce = s32[64]{0:T(128)S(1)} all-reduce(s32[64]{0:T(128)S(1)} %dynamic-update-slice), channel_id=1, replica_groups=mesh['dp'=2,'expert'=16] {'expert'}, use_global_device_ids=true, to_apply=%add | all-reduce | flops 64 | bytes 512
  34.3 0.2 copy.30
  34.5 0.0 copy-start.3
  34.6 0.0 copy-done.5
  34.6 0.1 fusion.27
  34.7 0.1 reduce_window_sum.11
  34.7 0.2 select_reduce_fusion
  34.9 0.1 eq.93
  35.0 0.1 copy.33
  35.1 0.1 broadcast_compare_fusion
  35.2 0.0 all-to-all-done
  35.2 0.5 fusion.16
  35.7 30.0 %psum.7 = f32[64,16]{0,1:T(8,128)S(1)} all-reduce(f32[64,16]{0,1:T(8,128)S(1)} %fusion.16), channel_id=1, replica_groups=mesh['dp'=2,'expert'=16] {'expert'}, use_global_device_ids=true, to_apply=%region_3.4 | all-reduce | flops 1024 | bytes 8192 | tf_op jit(solution)/shard_map/psum | solution.py:73
  65.7 0.0 copy-start.2
  65.7 2.1 fusion.32
  67.8 1.1 convolution_add_fusion
  68.9 0.0 all-reduce.5.cloned.1.call-update
  68.9 0.1 iota_compare_fusion.2
  69.0 0.1 and_reduce_fusion
  69.1 0.1 copy.35
  69.3 0.1 reshape.121
  70.0 87.0 %all-reduce.5.cloned.1.call-done = f32[64,2048]{1,0:T(8,128)} async-done(((f32[64,2048]{1,0:T(8,128)}), f32[64,2048]{1,0:T(8,128)}) %all-reduce.5.cloned.1.call-update) | async-done | bytes 524304
  157.0 1.0 multiply_reduce_fusion
  158.0 0.9 fusion.28
  158.9 4.4 %all-gather = bf16[2,4,2048]{2,1,0:T(4,128)(2,1)S(1)} all-gather(bf16[1,4,2048]{2,1,0:T(4,128)(2,1)S(1)} %fusion.28), channel_id=1, replica_groups=mesh['dp'=2,'expert'=16] {'dp'}, dimensions={0}, use_global_device_ids=true | all-gather | bytes 49152 | tf_op jit(solution)/shard_map/all_gather | solution.py:94
  163.3 0.3 convolution_convert_fusion.1
  163.7 0.1 reshape.122
  163.8 19.2 %all_to_all.26 = bf16[16,6,2048]{2,1,0:T(8,128)(2,1)S(1)} all-to-all(bf16[16,6,2048]{2,1,0:T(8,128)(2,1)S(1)} %reshape.122), channel_id=1, replica_groups=mesh['dp'=2,'expert'=16] {'expert'}, dimensions={0} | all-to-all | bytes 786432 | tf_op jit(solution)/shard_map/all_to_all | solution.py:119
  183.0 0.1 reshape.123
  183.2 0.0 copy-start.8
  183.2 2.2 fusion.5
  185.4 0.0 copy-done.8
  185.4 0.5 fusion.13
  185.9 0.0 copy-start.6
  185.9 0.0 copy-start.10
  186.0 0.8 convolution_convert_fusion
  186.7 1.0 copy.37
  187.8 4.2 %all-to-all-start.2 = ((bf16[16,6,2048]{2,1,0:T(8,128)(2,1)}), bf16[16,6,2048]{2,1,0:T(8,128)(2,1)S(1)}, u32[]{:S(2)}, u32[]{:S(2)}) async-start(bf16[16,6,2048]{2,1,0:T(8,128)(2,1)} %copy.37), calls=%async_computation.2 | async-start | bytes 1048576 | tf_op jit(solution)/shard_map/all_to_all | solution.py:122
  191.9 0.0 copy-done.6
  191.9 0.1 copy.34
  192.0 0.6 dynamic-slice.3
  193.3 0.1 fusion.24
  193.4 12.8 %all-to-all-done.2 = bf16[16,6,2048]{2,1,0:T(8,128)(2,1)S(1)} async-done(((bf16[16,6,2048]{2,1,0:T(8,128)(2,1)}), bf16[16,6,2048]{2,1,0:T(8,128)(2,1)S(1)}, u32[]{:S(2)}, u32[]{:S(2)}) %all-to-all-start.2) | async-done | bytes 393248 | tf_op jit(solution)/shard_map/all_to_all | solution.py:122
  206.2 0.6 fusion.1
  206.8 8.3 %all-reduce.2 = bf16[8,2048]{1,0:T(8,128)(2,1)S(1)} all-reduce(bf16[8,2048]{1,0:T(8,128)(2,1)S(1)} %fusion.1), channel_id=3, replica_groups=mesh['dp'=2,'expert'=16] {'dp'}, use_global_device_ids=true, to_apply=%region_10.11.clone | all-reduce | flops 16384 | bytes 65536
  215.1 1.5 add_convert_fusion
  (19 shorter events, 0.2 us)
Async XLA Ops:
  6.5 179.4 %copy-start = (bf16[1,2048,512]{2,1,0:T(8,128)(2,1)S(1)}, bf16[1,2048,512]{2,1,0:T(8,128)(2,1)}, u32[]{:S(2)}) copy-start(bf16[1,2048,512]{2,1,0:T(8,128)(2,1)} %param.27) | copy-start | bytes 6291460
  9.6 10.7 %copy-start.4 = (s32[8,6]{1,0:T(8,128)S(1)}, s32[8,6]{1,0:T(8,128)}, u32[]{:S(2)}) copy-start(s32[8,6]{1,0:T(8,128)} %param.23) | copy-start | bytes 580
  9.6 10.8 %copy-start.7 = (u32[32]{0:T(128)S(1)}, u32[32]{0:T(128)}, u32[]{:S(2)}) copy-start(u32[32]{0:T(128)} %constant.49) | copy-start | bytes 388
  9.6 12.1 %copy-start.9 = (s32[4]{0:T(128)S(1)}, s32[4]{0:T(128)}, u32[]{:S(2)}) copy-start(s32[4]{0:T(128)} %param.18) | copy-start | bytes 52
  9.6 24.7 %copy-start.1 = (bf16[512,512]{1,0:T(8,128)(2,1)S(1)}, bf16[512,512]{1,0:T(8,128)(2,1)}, u32[]{:S(2)}) copy-start(bf16[512,512]{1,0:T(8,128)(2,1)} %param.20) | copy-start | bytes 1572868
  9.6 25.0 %copy-start.5 = (bf16[2048]{0:T(1024)(128)(2,1)S(1)}, bf16[2048]{0:T(1024)(128)(2,1)}, u32[]{:S(2)}) copy-start(bf16[2048]{0:T(1024)(128)(2,1)} %param.22) | copy-start | bytes 12292
  12.8 22.4 %all-to-all-start = ((bf16[4,16,512]{2,0,1:T(4,128)(2,1)}), bf16[4,16,512]{2,0,1:T(4,128)(2,1)S(1)}, u32[]{:S(2)}, u32[]{:S(2)}) async-start(bf16[4,16,512]{2,0,1:T(4,128)(2,1)} %copy.29), calls=%async_computation | async-start | bytes 131072 | tf_op jit(solution)/shard_map/all_to_all | solution.py:61
  20.2 136.8 %all-reduce.5.cloned.1.call-start = ((), (), s32[]{:S(2)}) async-start(), calls=%async_computation.3 | async-start | bytes 1048576
  34.5 33.3 %copy-start.3 = (bf16[32,2048]{1,0:T(8,128)(2,1)S(1)}, bf16[32,2048]{1,0:T(8,128)(2,1)}, u32[]{:S(2)}) copy-start(bf16[32,2048]{1,0:T(8,128)(2,1)} %param.21) | copy-start | bytes 393220
  65.7 91.3 %copy-start.2 = (bf16[4,2048]{1,0:T(4,128)(2,1)S(1)}, bf16[4,2048]{1,0:T(4,128)(2,1)}, u32[]{:S(2)}) copy-start(bf16[4,2048]{1,0:T(4,128)(2,1)} %param.17) | copy-start | bytes 49156
  183.2 2.2 copy-start.8
  185.9 6.0 %copy-start.6 = (f32[8,6]{1,0:T(8,128)S(1)}, f32[8,6]{1,0:T(8,128)}, u32[]{:S(2)}) copy-start(f32[8,6]{1,0:T(8,128)} %param.24) | copy-start | bytes 580
  185.9 6.1 %copy-start.10 = (u32[32]{0:T(128)S(1)}, u32[32]{0:T(128)}, u32[]{:S(2)}) copy-start(u32[32]{0:T(128)} %constant.59) | copy-start | bytes 388
  187.8 18.4 %all-to-all-start.2 = ((bf16[16,6,2048]{2,1,0:T(8,128)(2,1)}), bf16[16,6,2048]{2,1,0:T(8,128)(2,1)S(1)}, u32[]{:S(2)}, u32[]{:S(2)}) async-start(bf16[16,6,2048]{2,1,0:T(8,128)(2,1)} %copy.37), calls=%async_computation.2 | async-start | bytes 1048576 | tf_op jit(solution)/shard_map/all_to_all | solution.py:122
Sparse Core Ops, SparseCore 0:
  69.0 87.9 all-reduce.4
where the time goes:
time: 224 us; the launch traced here: 223 us
  waiting for transfers between devices  99.8 us (45%)
  blocking collectives  74.4 us (33%)
  between operations  15.6 us (7%)
  matrix products  12.3 us (5%)
  starting transfers between devices  11.6 us (5%)
  other arithmetic  5.19 us (2%)
  local copies, waits for them, and re-layouts  4.47 us (2%)
    unnamed x2, waiting for transfers between devices  87 us
    psum x1, blocking collectives, local(): adapter_down_rows = lax.psum(adapter_output, 'expert')  30 us
    unnamed x2, blocking collectives  20.7 us
    all_to_all x1, blocking collectives, local(): lax.all_to_all(outgoing, 'expert', split_axis=0, concat_axis=0, tiled=True)  19.2 us
    all_to_all x1, waiting for transfers between devices, local(): lax.all_to_all(partial_value.astype(jnp.bfloat16), 'expert', split_axis=0...  12.8 us
    all_to_all x1, starting transfers between devices, local(): lax.all_to_all(latent_out, 'expert', split_axis=1, concat_axis=0, tiled=T...  7.41 us
  transfers between devices with their start and end apart: 3, of which 2 were waited for; matrix products, arithmetic and copies ran while one was open for 1% of the time, Pallas kernels for 0%

commit v1 on v0

--- a/solution.py
+++ b/solution.py
@@ -70,7 +70,11 @@
     adapter_output = jnp.sum(
         jnp.where(chosen_adapters[:, :, None], down_projected_rows, 0.0), axis=1
     )
-    adapter_down_rows = lax.psum(adapter_output, "expert")
+    adapter_down_rows = adapter_output
+    for hop in (1, 2, 4, 8):
+        adapter_down_rows = adapter_down_rows + lax.ppermute(
+            adapter_down_rows, "expert", [(dev, dev ^ hop) for dev in range(16)]
+        )
     adapter_scaled_output = (ADAPTER_SCALE * adapter_down_rows).astype(jnp.bfloat16)
     first_owned = lax.axis_index("expert") * owned_count
     holder_mask = (

time: 224 us -> 205 us (0.915)
  blocking collectives: 74.4 us -> 44.4 us
  waiting for transfers between devices: 99.8 us -> 109 us
    psum x1 -> x0, blocking collectives: 30 us -> none  [local(): adapter_down_rows = lax.psum(adapter_output, 'expert')]
    ppermute x0 -> x4, waiting for transfers between devices: none -> 8.87 us  [local(): lax.ppermute(adapter_down_rows, 'expert', [(dev, dev ^ hop) for dev in ra...]
  transfers between devices with their start and end apart: 3 -> 7, of which waited for: 2 -> 6; matrix products, arithmetic and copies ran while one was open for 1% -> 2% of each run, Pallas kernels for 0% -> 0%
where the time goes in v1:
time: 205 us
  waiting for transfers between devices  109 us (53%)
  blocking collectives  44.4 us (22%)
  between operations  15.6 us (8%)
  starting transfers between devices  13.6 us (7%)
  matrix products  12.3 us (6%)
  other arithmetic  5.19 us (3%)
  local copies, waits for them, and re-layouts  4.47 us (2%)
    unnamed x2, waiting for transfers between devices  87.3 us
    unnamed x2, blocking collectives  20.7 us
    all_to_all x1, blocking collectives, local(): lax.all_to_all(outgoing, 'expert', split_axis=0, concat_axis=0, tiled=True)  19.2 us
    all_to_all x1, waiting for transfers between devices, local(): lax.all_to_all(partial_value.astype(jnp.bfloat16), 'expert', split_axis=0...  12.8 us
    ppermute x4, waiting for transfers between devices, local(): lax.ppermute(adapter_down_rows, 'expert', [(dev, dev ^ hop) for dev in ra...  8.87 us
    all_to_all x1, starting transfers between devices, local(): lax.all_to_all(latent_out, 'expert', split_axis=1, concat_axis=0, tiled=T...  7.41 us
    all_gather x1, blocking collectives, local(): column = lax.all_gather(normed, 'dp', axis=0, tiled=True)  4.41 us
    all_to_all x1, starting transfers between devices, local(): lax.all_to_all(partial_value.astype(jnp.bfloat16), 'expert', split_axis=0...  4.16 us
  transfers between devices with their start and end apart: 7, of which 6 were waited for; matrix products, arithmetic and copies ran while one was open for 2% of the time, Pallas kernels for 0%

profile of v1, /device:TPU:0, one launch (start us, length us, event | category | flops | bytes accessed | tf_op | source)
XLA Modules:
  0.0 204.5 jit_solution(9691120842002466263)
XLA Ops:
  6.5 0.9 iota_compare_fusion.4
  7.4 2.1 %fusion.17 = f32[4,16,512]{2,1,0:T(8,128)S(1)} fusion(bf16[4,16,576]{2,1,0:T(8,128)(2,1)} %param.14, bf16[4,512,576]{1,2,0:T(8,128)(2,1)} %param.15, pred[4,512]{1,0:T(4,128)(4,1)S(1)} %iota_compare_fusion.4), kind=kOutput, calls=%fused_computation.19 | convolution fusion | flops 37814272 | bytes 2566144 | tf_op jit(solution)/shard_map/vmap()/dot_general | solution.py:15
  9.6 0.0 copy-start.9
  9.6 0.0 copy-start.1
  9.6 0.0 copy-start.4
  9.6 0.2 fusion.31
  9.8 2.3 %fusion.19 = bf16[4,16,512]{2,1,0:T(8,128)(2,1)S(1)} fusion(bf16[4,512,576]{1,2,0:T(8,128)(2,1)} %param.15, f32[4,16]{1,0:T(4,128)S(1)} %fusion.31, f32[4,16,512]{2,1,0:T(8,128)S(1)} %fusion.17), kind=kOutput, calls=%fused_computation.21 | convolution fusion | flops 33686080 | bytes 2426880 | tf_op jit(solution)/shard_map/vmap()/dot_general | solution.py:25
  12.1 0.7 copy.29
  12.8 7.4 %all-to-all-start = ((bf16[4,16,512]{2,0,1:T(4,128)(2,1)}), bf16[4,16,512]{2,0,1:T(4,128)(2,1)S(1)}, u32[]{:S(2)}, u32[]{:S(2)}) async-start(bf16[4,16,512]{2,0,1:T(4,128)(2,1)} %copy.29), calls=%async_computation | async-start | bytes 131072 | tf_op jit(solution)/shard_map/all_to_all | solution.py:61
  20.2 0.0 all-reduce.5.cloned.1.call-start
  20.3 0.6 fusion.30
  21.5 0.2 dynamic-update-slice
  21.8 12.4 %all-reduce = s32[64]{0:T(128)S(1)} all-reduce(s32[64]{0:T(128)S(1)} %dynamic-update-slice), channel_id=1, replica_groups=mesh['dp'=2,'expert'=16] {'expert'}, use_global_device_ids=true, to_apply=%add | all-reduce | flops 64 | bytes 512
  34.1 0.2 copy.30
  34.4 0.0 copy-start.3
  34.4 0.1 eq.89
  34.5 0.1 fusion.27
  34.5 0.1 reduce_window_sum.11
  34.6 0.2 select_reduce_fusion
  34.8 0.1 eq.93
  34.9 0.1 copy.33
  35.0 0.0 all-to-all-done
  35.0 0.5 fusion.16
  35.5 0.1 collective-permute-start
  35.6 1.1 collective-permute-done
  36.7 0.9 collective-permute-start.1
  37.6 2.8 %collective-permute-done.1 = f32[64,16]{0,1:T(8,128)S(1)} collective-permute-done((f32[64,16]{0,1:T(8,128)S(1)}, f32[64,16]{0,1:T(8,128)S(1)}, u32[]{:S(2)}, u32[]{:S(2)}) %collective-permute-start.1) | collective-permute-done | bytes 4128 | tf_op jit(solution)/shard_map/ppermute | solution.py:75
  40.4 0.5 collective-permute-start.2
  40.9 0.1 broadcast_compare_fusion
  41.0 0.1 copy.32
  41.1 2.9 %collective-permute-done.2 = f32[64,16]{0,1:T(8,128)S(1)} collective-permute-done((f32[64,16]{0,1:T(8,128)S(1)}, f32[64,16]{0,1:T(8,128)S(1)}, u32[]{:S(2)}, u32[]{:S(2)}) %collective-permute-start.2) | collective-permute-done | bytes 4128 | tf_op jit(solution)/shard_map/ppermute | solution.py:75
  44.0 0.5 collective-permute-start.3
  44.6 2.1 %fusion.32 = f32[64,2048]{1,0:T(8,128)S(1)} fusion(bf16[64,512]{1,0:T(8,128)(2,1)S(1)} %all_to_all.20, bf16[512,2048]{1,0:T(8,128)(2,1)} %param.19), kind=kOutput, calls=%fused_computation.50 | convolution fusion | flops 134217728 | bytes 2686976 | tf_op jit(solution)/shard_map/dot_general | solution.py:87
  46.6 2.0 collective-permute-done.3
  48.7 1.1 convolution_add_fusion
  49.7 0.0 all-reduce.5.cloned.1.call-update
  49.8 0.1 iota_compare_fusion.2
  49.8 0.1 and_reduce_fusion
  49.9 0.1 copy.35
  50.1 0.1 reshape.121
  50.8 87.3 %all-reduce.5.cloned.1.call-done = f32[64,2048]{1,0:T(8,128)} async-done(((f32[64,2048]{1,0:T(8,128)}), f32[64,2048]{1,0:T(8,128)}) %all-reduce.5.cloned.1.call-update) | async-done | bytes 524304
  138.1 1.0 multiply_reduce_fusion
  139.1 0.9 fusion.28
  140.1 4.4 %all-gather = bf16[2,4,2048]{2,1,0:T(4,128)(2,1)S(1)} all-gather(bf16[1,4,2048]{2,1,0:T(4,128)(2,1)S(1)} %fusion.28), channel_id=1, replica_groups=mesh['dp'=2,'expert'=16] {'dp'}, dimensions={0}, use_global_device_ids=true | all-gather | bytes 49152 | tf_op jit(solution)/shard_map/all_gather | solution.py:98
  144.5 0.3 convolution_convert_fusion.1
  144.8 0.1 reshape.122
  144.9 19.2 %all_to_all.26 = bf16[16,6,2048]{2,1,0:T(8,128)(2,1)S(1)} all-to-all(bf16[16,6,2048]{2,1,0:T(8,128)(2,1)S(1)} %reshape.122), channel_id=1, replica_groups=mesh['dp'=2,'expert'=16] {'expert'}, dimensions={0} | all-to-all | bytes 786432 | tf_op jit(solution)/shard_map/all_to_all | solution.py:123
  164.2 0.1 reshape.123
  164.3 0.0 copy-start.8
  164.3 2.2 %fusion.5 = f32[96,512]{1,0:T(8,128)S(1)} fusion(bf16[96,2048]{1,0:T(8,128)(2,1)S(1)} %reshape.123, bf16[1,2048,512]{2,1,0:T(8,128)(2,1)} %param.25), kind=kOutput, calls=%fused_computation.9 | convolution fusion | flops 201326592 | bytes 2686976 | tf_op jit(solution)/shard_map/dot_general | solution.py:31
  166.5 0.0 copy-done.8
  166.5 0.5 fusion.13
  167.1 0.0 copy-start.6
  167.1 0.0 copy-start.10
  167.1 0.8 convolution_convert_fusion
  167.9 1.0 copy.37
  168.9 4.2 %all-to-all-start.2 = ((bf16[16,6,2048]{2,1,0:T(8,128)(2,1)}), bf16[16,6,2048]{2,1,0:T(8,128)(2,1)S(1)}, u32[]{:S(2)}, u32[]{:S(2)}) async-start(bf16[16,6,2048]{2,1,0:T(8,128)(2,1)} %copy.37), calls=%async_computation.2 | async-start | bytes 1048576 | tf_op jit(solution)/shard_map/all_to_all | solution.py:126
  173.1 0.1 copy.34
  173.2 0.6 dynamic-slice.3
  174.4 0.1 fusion.24
  174.5 12.8 %all-to-all-done.2 = bf16[16,6,2048]{2,1,0:T(8,128)(2,1)S(1)} async-done(((bf16[16,6,2048]{2,1,0:T(8,128)(2,1)}), bf16[16,6,2048]{2,1,0:T(8,128)(2,1)S(1)}, u32[]{:S(2)}, u32[]{:S(2)}) %all-to-all-start.2) | async-done | bytes 393248 | tf_op jit(solution)/shard_map/all_to_all | solution.py:126
  187.3 0.6 fusion.1
  187.9 8.3 %all-reduce.2 = bf16[8,2048]{1,0:T(8,128)(2,1)S(1)} all-reduce(bf16[8,2048]{1,0:T(8,128)(2,1)S(1)} %fusion.1), channel_id=3, replica_groups=mesh['dp'=2,'expert'=16] {'dp'}, use_global_device_ids=true, to_apply=%region_9.10.clone | all-reduce | flops 16384 | bytes 65536
  196.2 1.5 add_convert_fusion
  (29 shorter events, 0.2 us)
Async XLA Ops:
  6.5 160.5 %copy-start = (bf16[1,2048,512]{2,1,0:T(8,128)(2,1)S(1)}, bf16[1,2048,512]{2,1,0:T(8,128)(2,1)}, u32[]{:S(2)}) copy-start(bf16[1,2048,512]{2,1,0:T(8,128)(2,1)} %param.27) | copy-start | bytes 6291460
  9.6 10.7 %copy-start.7 = (u32[32]{0:T(128)S(1)}, u32[32]{0:T(128)}, u32[]{:S(2)}) copy-start(u32[32]{0:T(128)} %constant.49) | copy-start | bytes 388
  9.6 11.9 %copy-start.9 = (s32[4]{0:T(128)S(1)}, s32[4]{0:T(128)}, u32[]{:S(2)}) copy-start(s32[4]{0:T(128)} %param.18) | copy-start | bytes 52
  9.6 24.6 %copy-start.1 = (bf16[512,512]{1,0:T(8,128)(2,1)S(1)}, bf16[512,512]{1,0:T(8,128)(2,1)}, u32[]{:S(2)}) copy-start(bf16[512,512]{1,0:T(8,128)(2,1)} %param.20) | copy-start | bytes 1572868
  9.6 24.8 %copy-start.4 = (s32[8,6]{1,0:T(8,128)S(1)}, s32[8,6]{1,0:T(8,128)}, u32[]{:S(2)}) copy-start(s32[8,6]{1,0:T(8,128)} %param.23) | copy-start | bytes 580
  9.8 31.3 %copy-start.5 = (bf16[2048]{0:T(1024)(128)(2,1)S(1)}, bf16[2048]{0:T(1024)(128)(2,1)}, u32[]{:S(2)}) copy-start(bf16[2048]{0:T(1024)(128)(2,1)} %param.22) | copy-start | bytes 12292
  12.8 22.2 %all-to-all-start = ((bf16[4,16,512]{2,0,1:T(4,128)(2,1)}), bf16[4,16,512]{2,0,1:T(4,128)(2,1)S(1)}, u32[]{:S(2)}, u32[]{:S(2)}) async-start(bf16[4,16,512]{2,0,1:T(4,128)(2,1)} %copy.29), calls=%async_computation | async-start | bytes 131072 | tf_op jit(solution)/shard_map/all_to_all | solution.py:61
  20.2 118.0 %all-reduce.5.cloned.1.call-start = ((), (), s32[]{:S(2)}) async-start(), calls=%async_computation.3 | async-start | bytes 1048576
  34.4 14.3 %copy-start.3 = (bf16[32,2048]{1,0:T(8,128)(2,1)S(1)}, bf16[32,2048]{1,0:T(8,128)(2,1)}, u32[]{:S(2)}) copy-start(bf16[32,2048]{1,0:T(8,128)(2,1)} %param.21) | copy-start | bytes 393220
  35.5 1.2 collective-permute-start
  36.7 3.7 %collective-permute-start.1 = (f32[64,16]{0,1:T(8,128)S(1)}, f32[64,16]{0,1:T(8,128)S(1)}, u32[]{:S(2)}, u32[]{:S(2)}) collective-permute-start(f32[64,16]{0,1:T(8,128)S(1)} %add.51), channel_id=1, source_target_pairs={{0,2},{1,3},{2,0},{3,1},{4,6},{5,7},{6,4},{7,5},{8,10},{9,11},{10,... | collective-permute-start | bytes 12296 | tf_op jit(solution)/shard_map/ppermute | solution.py:75
  40.4 3.7 %collective-permute-start.2 = (f32[64,16]{0,1:T(8,128)S(1)}, f32[64,16]{0,1:T(8,128)S(1)}, u32[]{:S(2)}, u32[]{:S(2)}) collective-permute-start(f32[64,16]{0,1:T(8,128)S(1)} %add.52), channel_id=1, source_target_pairs={{0,4},{1,5},{2,6},{3,7},{4,0},{5,1},{6,2},{7,3},{8,12},{9,13},{10,... | collective-permute-start | bytes 12296 | tf_op jit(solution)/shard_map/ppermute | solution.py:75
  44.0 94.1 %copy-start.2 = (bf16[4,2048]{1,0:T(4,128)(2,1)S(1)}, bf16[4,2048]{1,0:T(4,128)(2,1)}, u32[]{:S(2)}) copy-start(bf16[4,2048]{1,0:T(4,128)(2,1)} %param.17) | copy-start | bytes 49156
  44.0 4.6 %collective-permute-start.3 = (f32[64,16]{0,1:T(8,128)S(1)}, f32[64,16]{0,1:T(8,128)S(1)}, u32[]{:S(2)}, u32[]{:S(2)}) collective-permute-start(f32[64,16]{0,1:T(8,128)S(1)} %add.53), channel_id=1, source_target_pairs={{0,8},{1,9},{2,10},{3,11},{4,12},{5,13},{6,14},{7,15},{8,0},{9,1},... | collective-permute-start | bytes 12296 | tf_op jit(solution)/shard_map/ppermute | solution.py:75
  164.3 2.2 %copy-start.8 = (bf16[1,2048,512]{2,1,0:T(8,128)(2,1)S(1)}, bf16[1,2048,512]{2,1,0:T(8,128)(2,1)}, u32[]{:S(2)}) copy-start(bf16[1,2048,512]{2,1,0:T(8,128)(2,1)} %param.26) | copy-start | bytes 6291460
  167.1 6.0 %copy-start.6 = (f32[8,6]{1,0:T(8,128)S(1)}, f32[8,6]{1,0:T(8,128)}, u32[]{:S(2)}) copy-start(f32[8,6]{1,0:T(8,128)} %param.24) | copy-start | bytes 580
  167.1 6.1 %copy-start.10 = (u32[32]{0:T(128)S(1)}, u32[32]{0:T(128)}, u32[]{:S(2)}) copy-start(u32[32]{0:T(128)} %constant.59) | copy-start | bytes 388
  168.9 18.4 %all-to-all-start.2 = ((bf16[16,6,2048]{2,1,0:T(8,128)(2,1)}), bf16[16,6,2048]{2,1,0:T(8,128)(2,1)S(1)}, u32[]{:S(2)}, u32[]{:S(2)}) async-start(bf16[16,6,2048]{2,1,0:T(8,128)(2,1)} %copy.37), calls=%async_computation.2 | async-start | bytes 1048576 | tf_op jit(solution)/shard_map/all_to_all | solution.py:126
Sparse Core Ops, SparseCore 0:
  49.9 88.2 all-reduce.4
